TPU v7x, 32 devices: a whole 2x2x4 slice. The times are simulated.
32 devices in a mesh: layer: 4 (over z), tile: 8 (over y, x, core).
Axes of the slice: x: 2, y: 2, z: 4, core: 2. Of those that a mesh axis runs over, the one named last changes fastest.
Arguments:
- leaf_rhs: float32 [4, 32, 128, 256], P('layer', 'tile'), may hold values from -6 to 6
- leaf_inv: float32 [4, 32, 128, 128], P('layer', 'tile'), as said below
- par_rhs: float32 [4, 16, 128, 256], P('layer', 'tile'), may hold values from -6 to 6
- par_inv: float32 [4, 16, 128, 128], P('layer', 'tile'), as said below
- top_rhs: float32 [16, 128, 256], P('tile', None, 'layer'), may hold values from -6 to 6
- top_inv: float32 [16, 128, 128], P('tile'), as said below
- leaf_tiles: float32 [4, 1280, 128, 128], P('layer', 'tile'), may hold values from -0.125 to 0.125
- leaf_cols: int32 [4, 1280], P('layer', 'tile'), may hold values from 0 to 3
- leaf_rows: int32 [4, 1280], P('layer', 'tile'), may hold values from 0 to 31, as said below
- leaf_count: int32 [4, 8], P('layer', 'tile'), may hold values from 1 to 160, as said below
- par_tiles: float32 [4, 640, 128, 128], P('layer', 'tile'), may hold values from -0.125 to 0.125
- par_cols: int32 [4, 640], P('layer', 'tile'), may hold values from 0 to 1
- par_rows: int32 [4, 640], P('layer', 'tile'), may hold values from 0 to 15
- par_count: int32 [4, 8], P('layer', 'tile'), may hold values from 1 to 80, as said below
Outputs:
- parent_solution: float32 [4, 16, 128, 256], P('layer', 'tile')
- top_solution: float32 [16, 128, 256], P('tile', None, 'layer')
Inputs may be any that keep to these rules, and one draw needn't show every extreme that they name: `leaf_inv`: lower triangular, diagonal entries of magnitude 0.5 to 2. `par_inv`: lower triangular, diagonal entries of magnitude 0.5 to 2. `top_inv`: lower triangular, diagonal entries of magnitude 0.5 to 2. `leaf_rows`: the elimination subtree of a lower-level supernode of owner o lies in o's group of owners: owners o and q share a group when o // 2 % (1) equals q // 2 % 1; a tile below 16 names an upper-level supernode held by an owner of the same group, and the top-level supernodes are ancestors of every subtree. `leaf_count`: some owner of every layer has a full list. `par_count`: some owner of every layer has a full list.
All inputs are finite; a program needn't handle non-finite values.
Results may differ from a plain program's by a relative error of at most 0.0003.
Values sent between devices are 32-bit elements; how exact they have to be, the bound alone decides.
No kernel may reach another device: no remote copies, remote signals or barrier semaphores. Data moves between devices by JAX's collectives and lax.ppermute only.
A program may use at most 128 MiB of HBM per device.

v0:
```python
import jax
import jax.numpy as jnp
from jax import lax
from jax.sharding import PartitionSpec as P


def tile_products(tiles, cols, count, solved):
    highest = lax.Precision.HIGHEST
    picked = jnp.take(solved, cols, axis=0)
    product = jnp.einsum("tij,tjk->tik", tiles, picked, precision=highest)
    slots = tiles.shape[0]
    in_use = jnp.arange(slots, dtype=jnp.int32) < count
    return (product.reshape(slots, -1), in_use)


def collect(targets_of, in_use, products, first, number):
    highest = lax.Precision.HIGHEST
    wanted = first + jnp.arange(number, dtype=jnp.int32)
    selector = jnp.logical_and(targets_of[None, :] == wanted[:, None], in_use[None, :]).astype(
        jnp.float32
    )
    return jnp.dot(selector, products, precision=highest, preferred_element_type=jnp.float32)


def local(
    leaf_rhs,
    leaf_inv,
    par_rhs,
    par_inv,
    top_rhs,
    top_inv,
    leaf_tiles,
    leaf_cols,
    leaf_rows,
    leaf_count,
    par_tiles,
    par_cols,
    par_rows,
    par_count,
):
    highest = lax.Precision.HIGHEST
    block = leaf_rhs.shape[2]
    columns = leaf_rhs.shape[3]
    owners = lax.axis_size("tile")
    parent_here = par_rhs.shape[1]
    parent_total = parent_here * owners
    top_total = top_inv.shape[0] * owners
    leaf_solution = jnp.einsum("bij,bjk->bik", leaf_inv[0], leaf_rhs[0], precision=highest)
    leaf_products, leaf_used = tile_products(
        leaf_tiles[0], leaf_cols[0], leaf_count[0, 0], leaf_solution
    )
    leaf_targets = leaf_rows[0]
    summed = collect(
        leaf_targets, leaf_used, leaf_products, jnp.int32(0), parent_here * lax.axis_size("tile")
    )
    parent_sum = lax.psum_scatter(
        summed.reshape(parent_here * lax.axis_size("tile"), block, columns),
        "tile",
        scatter_dimension=0,
        tiled=True,
    )
    parent_solution = jnp.einsum(
        "bij,bjk->bik", par_inv[0], par_rhs[0] - parent_sum, precision=highest
    )
    par_products, par_used = tile_products(
        par_tiles[0], par_cols[0], par_count[0, 0], parent_solution
    )
    top_local = collect(leaf_targets, leaf_used, leaf_products, parent_total, top_total)
    top_local = top_local + collect(par_rows[0], par_used, par_products, 0, top_total)
    top_local = top_local.reshape(top_total, block, columns)
    owned_rows = lax.psum_scatter(top_local, "tile", scatter_dimension=0, tiled=True)
    owned = lax.psum_scatter(owned_rows, "layer", scatter_dimension=2, tiled=True)
    top_solution = jnp.einsum("bij,bjk->bik", top_inv, top_rhs - owned, precision=highest)
    return (parent_solution[None], top_solution)


def solution(mesh):
    in_specs = (
        P("layer", "tile", None, None),
        P("layer", "tile", None, None),
        P("layer", "tile", None, None),
        P("layer", "tile", None, None),
        P("tile", None, "layer"),
        P("tile", None, None),
        P("layer", "tile", None, None),
        P("layer", "tile"),
        P("layer", "tile"),
        P("layer", "tile"),
        P("layer", "tile", None, None),
        P("layer", "tile"),
        P("layer", "tile"),
        P("layer", "tile"),
    )
    out_specs = (P("layer", "tile", None, None), P("tile", None, "layer"))
    return jax.shard_map(local, mesh=mesh, in_specs=in_specs, out_specs=out_specs, check_vma=False)
```

profile of v0, /device:TPU:0, one launch (start us, length us, event | category | flops | bytes accessed | tf_op | source)
XLA Modules:
  0.0 254.2 jit_solution(683817398950716475)
XLA Ops:
  7.2 0.0 copy-start
  7.2 0.0 reduce-scatter.4.cloned.1.call-start
  7.9 0.7 compare_select_fusion
  8.6 0.7 compare_and_fusion.1
  9.3 0.0 copy-done
  9.3 1.5 fusion.23
  10.9 8.6 %gather_fusion = f32[160,128,256]{2,1,0:T(8,128)} fusion(f32[4,128,256]{2,1,0:T(8,128)S(1)} %fusion.23, s32[1024]{0:T(1024)S(1)} %pad_clamp_fusion.1), kind=kCustom, calls=%fused_computation | custom fusion | bytes 41943680 | tf_op jit(solution)/shard_map/jit(_take)/gather | solution.py:9
  19.5 42.0 %fusion.10 = f32[160,128,256]{1,2,0:T(8,128)} fusion(f32[1,160,128,128]{3,2,1,0:T(8,128)} %param.20, f32[160,128,256]{2,1,0:T(8,128)} %gather_fusion, pred[160]{0:T(512)(128)(4,1)S(1)} %compare_and_fusion.1), kind=kOutput, calls=%fused_computation.13 | convolution fusion | flops 8058306560 | bytes 52428960 | tf_op jit(solution)/shard_map/tij,tjk->tik/dot_general | solution.py:10
  61.4 0.0 copy-start.6
  61.4 21.3 %copy.30 = f32[20,8,128,256]{3,1,2,0:T(8,128)} copy(f32[20,8,128,256]{2,3,1,0:T(8,128)} %bitcast.73) | data formatting | bytes 41943040
  82.8 0.0 copy-done.6
  82.8 0.0 copy-start.8
  82.8 11.0 %fusion = f32[16,128,256]{2,0,1:T(8,128)S(1)} fusion(s32[160]{0:T(256)S(1)} %bitcast.78, pred[160]{0:T(512)(128)(4,1)S(1)} %iota_compare_fusion.2, f32[20,8,128,256]{3,1,2,0:T(8,128)} %copy.30), kind=kOutput, calls=%fused_computation.3 | convolution fusion | flops 1006638080 | bytes 23069472 | tf_op jit(solution)/shard_map/dot_general | solution.py:22
  93.8 2.5 copy.27
  96.3 0.0 reduce-scatter.4.cloned.1.call-update
  96.3 0.0 reduce-scatter.6.cloned.1.call-start
  97.1 0.0 copy-done.8
  97.1 0.0 copy-start.2
  97.1 0.0 copy-start.3
  97.1 10.9 %fusion.32 = f32[16,32768]{1,0:T(8,128)S(1)} fusion(f32[160,32768]{1,0:T(8,128)} %bitcast.72, s32[160]{0:T(256)S(1)} %bitcast.79, s32[16]{0:T(128)S(1)} %iota_add_fusion, pred[160]{0:T(512)(128)(4,1)S(1)} %iota_compare_fusion.2), kind=kOutput, calls=%fused_computation.29 | convolution fusion | flops 1006638080 | bytes 23069536 | tf_op jit(solution)/shard_map/dot_general | solution.py:22
  108.1 32.3 %reduce-scatter.4.cloned.1.call-done = f32[2,128,256]{2,1,0:T(8,128)} async-done(((f32[16,128,256]{2,1,0:T(8,128)}), f32[2,128,256]{2,1,0:T(8,128)}) %reduce-scatter.4.cloned.1.call-update) | async-done | bytes 262160 | tf_op jit(solution)/shard_map/reduce_scatter | solution.py:56
  140.3 0.0 copy-done.2
  140.3 0.0 copy-done.3
  140.3 1.5 fusion.26
  141.9 5.0 %gather_fusion.1 = f32[80,128,256]{1,2,0:T(8,128)} fusion(f32[2,128,256]{1,2,0:T(8,128)S(1)} %bitcast.70, s32[1024]{0:T(1024)S(1)} %pad_clamp_fusion), kind=kCustom, calls=%fused_computation.1 | custom fusion | bytes 20971840 | tf_op jit(solution)/shard_map/jit(_take)/gather | solution.py:9
  146.9 14.9 %fusion.18 = f32[80,128,256]{1,2,0:T(8,128)} fusion(f32[1,80,128,128]{3,2,1,0:T(8,128)} %param.24, f32[80,128,256]{1,2,0:T(8,128)} %gather_fusion.1, pred[80]{0:T(512)(128)(4,1)S(1)} %compare_and_fusion), kind=kOutput, calls=%fused_computation.17 | convolution fusion | flops 4029153280 | bytes 26214480 | tf_op jit(solution)/shard_map/tij,tjk->tik/dot_general | solution.py:10
  161.8 0.0 copy-start.7
  161.8 11.6 %copy.31 = f32[10,8,128,256]{3,1,2,0:T(8,128)} copy(f32[10,8,128,256]{2,3,1,0:T(8,128)} %bitcast.74) | data formatting | bytes 20971520
  173.4 0.0 copy-start.1
  173.4 0.0 copy-done.7
  173.4 0.0 copy-start.4
  173.4 0.0 copy-start.5
  173.4 6.3 %convolution_add_fusion = f32[16,32768]{1,0:T(8,128)S(1)} fusion(f32[16,32768]{1,0:T(8,128)S(1)} %fusion.32, f32[80,32768]{1,0:T(8,128)} %bitcast.75, s32[80]{0:T(128)S(1)} %bitcast.82, pred[80]{0:T(512)(128)(4,1)S(1)} %iota_compare_fusion.3), kind=kOutput, calls=%fused_computation.2 | convolution fusion | flops 503843328 | bytes 14680464 | tf_op jit(solution)/shard_map/dot_general | solution.py:22
  179.8 0.6 copy.32
  180.4 1.9 copy.23
  182.3 0.0 reduce-scatter.6.cloned.1.call-update
  182.3 0.0 reduce-scatter.8.cloned.1.call-start
  182.4 41.2 %reduce-scatter.6.cloned.1.call-done = f32[2,128,256]{1,2,0:T(8,128)} async-done(((f32[16,128,256]{1,2,0:T(8,128)}), f32[2,128,256]{1,2,0:T(8,128)}) %reduce-scatter.6.cloned.1.call-update) | async-done | bytes 262160 | tf_op jit(solution)/shard_map/reduce_scatter | solution.py:71
  223.6 0.0 reduce-scatter.8.cloned.1.call-update
  223.6 0.8 copy.24
  224.4 21.4 %reduce-scatter.8.cloned.1.call-done = f32[2,128,64]{1,2,0:T(8,128)} async-done(((f32[2,128,256]{1,2,0:T(8,128)}), f32[2,128,64]{1,2,0:T(8,128)}) %reduce-scatter.8.cloned.1.call-update) | async-done | bytes 65552 | tf_op jit(solution)/shard_map/reduce_scatter | solution.py:72
  245.8 0.0 copy-done.4
  245.8 0.0 copy-done.5
  245.8 1.8 convolution_bitcast_fusion
  247.7 0.0 copy-done.1
  (7 shorter events, 0.0 us)
Async XLA Ops:
  7.2 2.2 copy-start
  7.2 133.2 %reduce-scatter.4.cloned.1.call-start = ((), (), s32[]{:S(2)}) async-start(), calls=%async_computation.3 | async-start | bytes 2359296 | tf_op jit(solution)/shard_map/reduce_scatter | solution.py:56
  61.4 21.3 %copy-start.6 = (s32[1,160]{1,0:T(1,128)S(1)}, s32[1,160]{1,0:T(1,128)}, u32[]{:S(2)}) copy-start(s32[1,160]{1,0:T(1,128)} %param.22) | copy-start | bytes 1924
  82.8 14.3 %copy-start.8 = (s32[1,80]{1,0:T(1,128)S(1)}, s32[1,80]{1,0:T(1,128)}, u32[]{:S(2)}) copy-start(s32[1,80]{1,0:T(1,128)} %param.25) | copy-start | bytes 964
  96.3 127.2 %reduce-scatter.6.cloned.1.call-start = ((), (), s32[]{:S(2)}) async-start(), calls=%async_computation.4 | async-start | bytes 2359296 | tf_op jit(solution)/shard_map/reduce_scatter | solution.py:71
  97.1 43.2 %copy-start.2 = (f32[1,2,128,256]{3,2,1,0:T(8,128)S(1)}, f32[1,2,128,256]{3,2,1,0:T(8,128)}, u32[]{:S(2)}) copy-start(f32[1,2,128,256]{3,2,1,0:T(8,128)} %param.16) | copy-start | bytes 786436
  97.1 43.2 %copy-start.3 = (f32[1,2,128,128]{3,2,1,0:T(8,128)S(1)}, f32[1,2,128,128]{3,2,1,0:T(8,128)}, u32[]{:S(2)}) copy-start(f32[1,2,128,128]{3,2,1,0:T(8,128)} %param.17) | copy-start | bytes 393220
  161.8 11.6 %copy-start.7 = (s32[1,80]{1,0:T(1,128)S(1)}, s32[1,80]{1,0:T(1,128)}, u32[]{:S(2)}) copy-start(s32[1,80]{1,0:T(1,128)} %param.26) | copy-start | bytes 964
  173.4 74.3 %copy-start.1 = (f32[1,4,128,256]{3,2,1,0:T(8,128)S(1)}, f32[1,4,128,256]{3,2,1,0:T(8,128)}, u32[]{:S(2)}) copy-start(f32[1,4,128,256]{3,2,1,0:T(8,128)} %param.14) | copy-start | bytes 1572868
  173.4 72.4 %copy-start.4 = (f32[2,128,128]{2,1,0:T(8,128)S(1)}, f32[2,128,128]{2,1,0:T(8,128)}, u32[]{:S(2)}) copy-start(f32[2,128,128]{2,1,0:T(8,128)} %param.19) | copy-start | bytes 393220
  173.4 72.4 %copy-start.5 = (f32[2,128,64]{1,2,0:T(8,128)S(1)}, f32[2,128,64]{1,2,0:T(8,128)}, u32[]{:S(2)}) copy-start(f32[2,128,64]{1,2,0:T(8,128)} %param.18) | copy-start | bytes 196612
  182.3 63.5 %reduce-scatter.8.cloned.1.call-start = ((), (), s32[]{:S(2)}) async-start(), calls=%async_computation.5 | async-start | bytes 327680 | tf_op jit(solution)/shard_map/reduce_scatter | solution.py:72
Sparse Core Ops, SparseCore 0:
  96.5 43.8 reduce-scatter.3
  182.4 41.0 reduce-scatter.5
  225.8 19.9 reduce-scatter.7
where the time goes:
time: 255 us; the launch traced here: 254 us
  waiting for transfers between devices  95 us (37%)
  matrix products  90 us (35%)
  local copies, waits for them, and re-layouts  52.5 us (21%)
  between operations  15.2 us (6%)
    dot_general x2, matrix products, tile_products(): product = jnp.einsum('tij,tjk->tik', tiles, picked, precision=highest)  56.8 us
    reduce_scatter x1, waiting for transfers between devices, local(): lax.psum_scatter(top_local, 'tile', scatter_dimension=0, tiled=True)  41.2 us
    unnamed x22, local copies, waits for them, and re-layouts  34.4 us
    reduce_scatter x1, waiting for transfers between devices, local(): lax.psum_scatter(summed.reshape(parent_here * lax.axis_size('tile'), bloc...  32.3 us
    dot_general x3, matrix products, collect(): jnp.dot(selector, products, precision=highest, preferred_element_type=jnp...  28.3 us
    reduce_scatter x1, waiting for transfers between devices, local(): lax.psum_scatter(owned_rows, 'layer', scatter_dimension=2, tiled=True)  21.4 us
    gather x2, local copies, waits for them, and re-layouts, tile_products(): picked = jnp.take(solved, cols, axis=0)  13.7 us
  transfers between devices with their start and end apart: 3, of which 3 were waited for; matrix products, arithmetic and copies ran while one was open for 5% of the time, Pallas kernels for 0%

commit v1 on v0

v1 whole, which is shorter than its diff:
```python
import functools
import math

import jax
import jax.numpy as jnp
from jax import lax
from jax.experimental import pallas as pl
from jax.experimental.pallas import tpu as pltpu
from jax.sharding import PartitionSpec as P

F32 = jnp.float32
BF16 = jnp.bfloat16


def split(value):
    high = value.astype(BF16)
    low = (value - high.astype(F32)).astype(BF16)
    return high, low


def dot(left, right):
    return jnp.dot(left, right, preferred_element_type=F32)


def dot3(left, right):
    left_high, left_low = left
    right_high, right_low = right
    return dot(left_high, right_high) + (dot(left_high, right_low) + dot(left_low, right_high))


def bits_of(number):
    bits = number.bit_length() - 1
    assert 1 << bits == number
    return bits


def slot_of(target, me, owners, per):
    owner = lax.div(target, jnp.int32(per))
    place = lax.rem(target, jnp.int32(per))
    relative = owner ^ me
    core = relative & 1
    rest = relative >> 1
    width = bits_of(owners) - 1
    turned = jnp.int32(0)
    for bit in range(width):
        turned = turned | (((rest >> bit) & 1) << (width - 1 - bit))
    where = jnp.where(place < per // 2, turned, rest)
    return (core * per + place) * (owners // 2) + where


def chunk_of(slots):
    return max(size for size in range(1, 17) if slots % size == 0)


def accumulate(rows_ref, cols_ref, count, first, number, me, owners, per, tiles_hbm, buf, acc, sems):
    slots = buf.shape[0]
    chunk = chunk_of(slots)

    def batch(g, _):
        @pl.when(g * chunk < count)
        def _():
            part = pl.ds(g * chunk, chunk)
            pltpu.make_async_copy(tiles_hbm.at[0, part], buf.at[part], sems.at[g]).wait()

            def one(s, _):
                row = rows_ref[0, s] - first

                @pl.when(jnp.logical_and(row >= 0, row < number))
                def _():
                    slot = slot_of(row, me, owners, per)
                    col = cols_ref[0, s]
                    acc[slot, col] = acc[slot, col] + buf[s]

                return 0

            lax.fori_loop(g * chunk, jnp.minimum((g + 1) * chunk, count), one, 0)

        return 0

    lax.fori_loop(0, slots // chunk, batch, 0)


def start_tiles(count, tiles_hbm, buf, sems):
    slots = buf.shape[0]
    chunk = chunk_of(slots)
    for g in range(slots // chunk):
        @pl.when(g * chunk < count)
        def _():
            part = pl.ds(g * chunk, chunk)
            pltpu.make_async_copy(tiles_hbm.at[0, part], buf.at[part], sems.at[g]).start()


def clear(acc):
    def one(k, _):
        acc[k] = jnp.zeros(acc.shape[1:], F32)
        return 0

    lax.fori_loop(0, acc.shape[0], one, 0)


def leaf_kernel(first, number, owners, per, me_ref, rows_ref, cols_ref, count_ref, inv_hbm, rhs_hbm, tiles_hbm,
                send_ref, keep_ref, buf, acc, inv, rhs, x_high, x_low, a_high, a_low, sems, small_sems):
    me = me_ref[0]
    count = count_ref[0, 0]
    inv_copy = pltpu.make_async_copy(inv_hbm.at[0], inv, small_sems.at[0])
    rhs_copy = pltpu.make_async_copy(rhs_hbm.at[0], rhs, small_sems.at[1])
    inv_copy.start()
    rhs_copy.start()
    start_tiles(count, tiles_hbm, buf, sems)
    clear(acc)
    inv_copy.wait()
    rhs_copy.wait()
    sources, block, _ = inv.shape
    for b in range(sources):
        high, low = split(dot3(split(inv[b]), split(rhs[b])))
        x_high[b * block:(b + 1) * block] = high
        x_low[b * block:(b + 1) * block] = low
    accumulate(rows_ref, cols_ref, count, first, number, me, owners, per, tiles_hbm, buf, acc, sems)
    group = a_high.shape[0] // block
    half = number // 2
    for side, out in ((1, send_ref), (0, keep_ref)):
        def some(g, _):
            for k in range(group):
                for b in range(sources):
                    high, low = split(acc[side * half + g * group + k, b])
                    a_high[k * block:(k + 1) * block, b * block:(b + 1) * block] = high
                    a_low[k * block:(k + 1) * block, b * block:(b + 1) * block] = low
            product = dot3((a_high[...], a_low[...]), (x_high[...], x_low[...]))
            out[pl.ds(g * group, group)] = product.reshape(group, block, -1)
            return 0

        lax.fori_loop(0, half // group, some, 0)


def whole(count):
    return [pl.BlockSpec(memory_space=pltpu.VMEM)] * count


def scalars(count):
    return [pl.BlockSpec(memory_space=pltpu.SMEM)] * count


def hbm(count):
    return [pl.BlockSpec(memory_space=pl.ANY)] * count


def leaf_products(me, rows, cols, count, inv, rhs, tiles, first, number, owners, per, name):
    slots, block = tiles.shape[1], tiles.shape[2]
    sources, columns = rhs.shape[1], rhs.shape[3]
    half = number // 2
    group = math.gcd(half, 4)
    out = jax.ShapeDtypeStruct((half, block, columns), F32)
    flops = 6 * number * block * sources * block * columns
    vmem = 4 * block * block * (slots + (number + 4) * sources) + 12 * number * block * columns + (6 << 20)
    return pl.pallas_call(
        functools.partial(leaf_kernel, first, number, owners, per),
        name=name,
        out_shape=(out, out),
        in_specs=scalars(4) + hbm(3),
        out_specs=tuple(whole(2)),
        scratch_shapes=[
            pltpu.VMEM((slots, block, block), F32),
            pltpu.VMEM((number, sources, block, block), F32),
            pltpu.VMEM(inv.shape[1:], F32),
            pltpu.VMEM(rhs.shape[1:], F32),
            pltpu.VMEM((sources * block, columns), BF16),
            pltpu.VMEM((sources * block, columns), BF16),
            pltpu.VMEM((group * block, sources * block), BF16),
            pltpu.VMEM((group * block, sources * block), BF16),
            pltpu.SemaphoreType.DMA((slots // chunk_of(slots),)),
            pltpu.SemaphoreType.DMA((2,)),
        ],
        compiler_params=pltpu.CompilerParams(vmem_limit_bytes=min(vmem, 60 << 20)),
        cost_estimate=pl.CostEstimate(flops=flops, bytes_accessed=tiles.size * 4, transcendentals=0),
    )(me, rows, cols, count, inv, rhs, tiles)


def parent_sum_kernel(number, owners, per, me_ref, rows_ref, cols_ref, count_ref, tiles_hbm, top_inv_ref, top_rhs_ref,
                      high_ref, low_ref, base_ref, buf, acc, sems):
    me = me_ref[0]
    count = count_ref[0, 0]
    start_tiles(count, tiles_hbm, buf, sems)
    clear(acc)
    for t in range(top_inv_ref.shape[0]):
        left = split(top_inv_ref[t])
        base_ref[t] = dot3(left, split(top_rhs_ref[t].T)).T
    accumulate(rows_ref, cols_ref, count, 0, number, me, owners, per, tiles_hbm, buf, acc, sems)
    sources, block = acc.shape[1], acc.shape[2]

    def one(k, _):
        for b in range(sources):
            high, low = split(acc[k, b])
            high_ref[k, :, b * block:(b + 1) * block] = high
            low_ref[k, :, b * block:(b + 1) * block] = low
        return 0

    lax.fori_loop(0, number, one, 0)


def parent_sums(me, rows, cols, count, tiles, top_inv, top_rhs, sources, number, owners, per):
    slots, block = tiles.shape[1], tiles.shape[2]
    half = jax.ShapeDtypeStruct((number, block, sources * block), BF16)
    vmem = 4 * block * block * (slots + 2 * number * sources) + (6 << 20)
    return pl.pallas_call(
        functools.partial(parent_sum_kernel, number, owners, per),
        name="parent_sums",
        out_shape=(half, half, jax.ShapeDtypeStruct(top_rhs.shape, F32)),
        in_specs=scalars(4) + hbm(1) + whole(2),
        out_specs=tuple(whole(3)),
        scratch_shapes=[
            pltpu.VMEM((slots, block, block), F32),
            pltpu.VMEM((number, sources, block, block), F32),
            pltpu.SemaphoreType.DMA((slots // chunk_of(slots),)),
        ],
        compiler_params=pltpu.CompilerParams(vmem_limit_bytes=min(vmem, 60 << 20)),
        cost_estimate=pl.CostEstimate(flops=tiles.size, bytes_accessed=tiles.size * 4, transcendentals=0),
    )(me, rows, cols, count, tiles, top_inv, top_rhs)


def parent_kernel(parts, rhs_ref, inv_ref, high_ref, low_ref, send_leaf_ref, keep_leaf_ref, *refs):
    pieces, (solution_ref, send_ref, keep_ref, p_high, p_low) = refs[:2 * parts], refs[2 * parts:]
    per, block, _ = rhs_ref.shape
    place = 0
    for part in range(parts):
        mine, other = pieces[2 * part], pieces[2 * part + 1]
        for k in range(mine.shape[0]):
            right = rhs_ref[place] - (mine[k] + other[k])
            solved = dot3(split(inv_ref[place]), split(right))
            solution_ref[place] = solved
            high, low = split(solved)
            p_high[place * block:(place + 1) * block] = high
            p_low[place * block:(place + 1) * block] = low
            place += 1
    half = send_ref.shape[0]
    group = math.gcd(half, 4)
    for side, leaf, out in ((1, send_leaf_ref, send_ref), (0, keep_leaf_ref, keep_ref)):
        def some(g, _):
            part = pl.ds(side * half + g * group, group)
            high = high_ref[part].reshape(group * block, -1)
            low = low_ref[part].reshape(group * block, -1)
            product = dot3((high, low), (p_high[...], p_low[...]))
            here = pl.ds(g * group, group)
            out[here] = leaf[here] + product.reshape(group, block, -1)
            return 0

        lax.fori_loop(0, half // group, some, 0)


def parent_products(rhs, inv, high, low, send_leaf, keep_leaf, pieces):
    per, block, columns = rhs.shape
    out = jax.ShapeDtypeStruct(send_leaf.shape, F32)
    flops = 6 * high.size * columns
    return pl.pallas_call(
        functools.partial(parent_kernel, len(pieces) // 2),
        name="parent_products",
        out_shape=(jax.ShapeDtypeStruct(rhs.shape, F32), out, out),
        in_specs=whole(6 + len(pieces)),
        out_specs=tuple(whole(3)),
        scratch_shapes=[pltpu.VMEM((per * block, columns), BF16)] * 2,
        compiler_params=pltpu.CompilerParams(vmem_limit_bytes=(8 << 20) + 16 * send_leaf.size + 4 * high.size),
        cost_estimate=pl.CostEstimate(flops=flops, bytes_accessed=4 * high.size, transcendentals=0),
    )(rhs, inv, high, low, send_leaf, keep_leaf, *pieces)


def top_kernel(parts, layers, layer_ref, inv_ref, *refs):
    pieces, (out_ref, turned) = refs[:2 * parts], refs[2 * parts:]
    width = out_ref.shape[2]
    layer = layer_ref[0]
    place = 0
    for part in range(parts):
        mine, other = pieces[2 * part], pieces[2 * part + 1]
        for k in range(mine.shape[0]):
            turned[...] = dot3(split(inv_ref[place]), split(mine[k] + other[k])).T
            for d in range(layers):
                start = pl.multiple_of((layer ^ d) * width, width)
                out_ref[d, place] = turned[pl.ds(start, width)]
            place += 1


def top_products(layer, inv, pieces, layers):
    per, block, _ = inv.shape
    columns = pieces[0].shape[2]
    return pl.pallas_call(
        functools.partial(top_kernel, len(pieces) // 2, layers),
        name="top_products",
        out_shape=jax.ShapeDtypeStruct((layers, per, columns // layers, block), F32),
        in_specs=scalars(1) + whole(1 + len(pieces)),
        out_specs=whole(1)[0],
        scratch_shapes=[pltpu.VMEM((columns, block), F32)],
        compiler_params=pltpu.CompilerParams(vmem_limit_bytes=8 << 20),
        cost_estimate=pl.CostEstimate(flops=6 * inv.size * columns, bytes_accessed=inv.size * 4, transcendentals=0),
    )(layer, inv, *pieces)


def exchange(value, axis, mask):
    size = lax.axis_size(axis)
    return lax.ppermute(value, axis, [(i, i ^ mask) for i in range(size)])


def scatter_sum(send, keep, owners, per):
    got = exchange(send, "tile", 1)
    rest = owners // 2
    halves = [(0, per // 2), (per // 2, per)] if per > 1 else [(0, per)]
    orders = [[1 << bit for bit in range(1, bits_of(owners))]]
    orders.append(orders[0][::-1])
    if per == 1:
        orders = orders[1:]
    shape = (per, rest) + send.shape[1:]
    keep, got = keep.reshape(shape), got.reshape(shape)
    state = []
    for low, high in halves:
        state.append((keep[low:high], got[low:high]))
    for step in range(bits_of(rest)):
        sent = []
        for (mine, other), order in zip(state, orders):
            cut = mine.shape[1] // 2
            sent.append(exchange(mine[:, cut:] + other[:, cut:], "tile", order[step]))
        state = [
            (mine[:, : mine.shape[1] // 2] + other[:, : mine.shape[1] // 2], new)
            for (mine, other), new in zip(state, sent)
        ]
    pieces = []
    for mine, other in state:
        pieces += [mine[:, 0], other[:, 0]]
    return pieces


def local(leaf_rhs, leaf_inv, par_rhs, par_inv, top_rhs, top_inv, leaf_tiles, leaf_cols, leaf_rows, leaf_count,
          par_tiles, par_cols, par_rows, par_count):
    owners, layers = lax.axis_size("tile"), lax.axis_size("layer")
    per, top_per = par_rhs.shape[1], top_inv.shape[0]
    parents, tops = per * owners, top_per * owners
    me = lax.axis_index("tile").astype(jnp.int32).reshape(1)
    layer = lax.axis_index("layer").astype(jnp.int32).reshape(1)
    leaf = (me, leaf_rows, leaf_cols, leaf_count, leaf_inv, leaf_rhs, leaf_tiles)
    send, keep = leaf_products(*leaf, 0, parents, owners, per, "leaf_to_parents")
    pieces = scatter_sum(send, keep, owners, per)
    send_leaf, keep_leaf = leaf_products(*leaf, parents, tops, owners, top_per, "leaf_to_tops")
    top_rhs_turned = jnp.transpose(top_rhs, (0, 2, 1))
    high, low, base = parent_sums(
        me, par_rows, par_cols, par_count, par_tiles, top_inv, top_rhs_turned, per, tops, owners, top_per
    )
    solved, send, keep = parent_products(par_rhs[0], par_inv[0], high, low, send_leaf, keep_leaf, pieces)
    pieces = scatter_sum(send, keep, owners, top_per)
    chunks = top_products(layer, top_inv, pieces, layers)
    total = base - chunks[0]
    others = [exchange(chunks[d], "layer", d) for d in range(1, layers)]
    for other in others:
        total = total - other
    return solved[None], jnp.transpose(total, (0, 2, 1))


def solution(mesh):
    spread = P("layer", "tile", None, None)
    lists = P("layer", "tile")
    in_specs = (spread, spread, spread, spread, P("tile", None, "layer"), P("tile", None, None), spread, lists, lists,
                lists, spread, lists, lists, lists)
    out_specs = (spread, P("tile", None, "layer"))
    return jax.shard_map(local, mesh=mesh, in_specs=in_specs, out_specs=out_specs, check_vma=False)
```

time: 255 us -> 69.9 us (0.27)
  matrix products: 90 us -> 0 us
  waiting for transfers between devices: 95 us -> 22.3 us
  local copies, waits for them, and re-layouts: 52.5 us -> 7.64 us
  starting transfers between devices: 0.12 us -> 21.9 us
  Pallas kernels: 0 us -> 14.2 us
  between operations: 15.2 us -> 2.17 us
    reduce_scatter x3 -> x0, waiting for transfers between devices: 94.9 us -> none  [the longest x1 41.2 us: local(): lax.psum_scatter(top_local, 'tile', scatter_dimension=0, tiled=True)]
    dot_general x8 -> x0, matrix products: 90 us -> none  [the longest x2 56.8 us: tile_products(): product = jnp.einsum('tij,tjk->tik', tiles, picked, precision=highest)]
    unnamed x22 -> x24, local copies, waits for them, and re-layouts: 34.4 us -> 7.35 us
    ppermute x0 -> x13, waiting for transfers between devices: none -> 22.3 us  [exchange(): return lax.ppermute(value, axis, [(i, i ^ mask) for i in range(size)])]
    ppermute x0 -> x13, starting transfers between devices: none -> 21.9 us  [exchange(): return lax.ppermute(value, axis, [(i, i ^ mask) for i in range(size)])]
    pallas_call x0 -> x5, Pallas kernels: none -> 14.2 us  [the longest x2 9.82 us: leaf_products(): pl.pallas_call(functools.partial(leaf_kernel, first, number, owners, per)...]
    gather x2 -> x0, local copies, waits for them, and re-layouts: 13.7 us -> none  [tile_products(): picked = jnp.take(solved, cols, axis=0)]
  transfers between devices with their start and end apart: 3 -> 13, of which waited for: 3 -> 11; matrix products, arithmetic and copies ran while one was open for 5% -> 1% of each run, Pallas kernels for 0% -> 10%
where the time goes in v1:
time: 69.9 us; the launch traced here: 69.3 us
  waiting for transfers between devices  22.3 us (32%)
  starting transfers between devices  21.9 us (31%)
  Pallas kernels  14.2 us (20%)
  local copies, waits for them, and re-layouts  7.64 us (11%)
  between operations  2.17 us (3%)
  other arithmetic  1.06 us (2%)
    ppermute x13, waiting for transfers between devices, exchange(): return lax.ppermute(value, axis, [(i, i ^ mask) for i in range(size)])  22.3 us
    ppermute x13, starting transfers between devices, exchange(): return lax.ppermute(value, axis, [(i, i ^ mask) for i in range(size)])  21.9 us
    pallas_call x2, Pallas kernels, leaf_products(): pl.pallas_call(functools.partial(leaf_kernel, first, number, owners, per)...  9.82 us
    unnamed x24, local copies, waits for them, and re-layouts  7.35 us
    pallas_call x1, Pallas kernels, parent_products(): pl.pallas_call(functools.partial(parent_kernel, len(pieces) // 2), name='...  2.13 us
    pallas_call x1, Pallas kernels, parent_sums(): pl.pallas_call(functools.partial(parent_sum_kernel, number, owners, per),...  1.89 us
  transfers between devices with their start and end apart: 13, of which 11 were waited for; matrix products, arithmetic and copies ran while one was open for 1% of the time, Pallas kernels for 10%

profile of v1, /device:TPU:0, one launch (start us, length us, event | category | flops | bytes accessed | tf_op | source)
XLA Modules:
  0.0 69.3 jit_solution(250589135198451255)
XLA Ops:
  0.6 0.0 copy-start.10
  1.3 4.0 %copy-done = f32[1,160,128,128]{3,2,1,0:T(8,128)S(1)} copy-done((f32[1,160,128,128]{3,2,1,0:T(8,128)S(1)}, f32[1,160,128,128]{3,2,1,0:T(8,128)}, u32[]{:S(2)}) %copy-start) | copy-done | bytes 10485784
  5.3 1.0 %copy-done.2 = f32[1,4,128,256]{3,2,1,0:T(8,128)S(1)} copy-done((f32[1,4,128,256]{3,2,1,0:T(8,128)S(1)}, f32[1,4,128,256]{3,2,1,0:T(8,128)}, u32[]{:S(2)}) %copy-start.2) | copy-done | bytes 524312
  6.3 0.9 %copy-done.3 = f32[1,4,128,128]{3,2,1,0:T(8,128)S(1)} copy-done((f32[1,4,128,128]{3,2,1,0:T(8,128)S(1)}, f32[1,4,128,128]{3,2,1,0:T(8,128)}, u32[]{:S(2)}) %copy-start.3) | copy-done | bytes 262168
  7.3 0.7 copy-done.8
  8.0 0.7 copy-done.9
  8.7 4.9 %leaf_to_parents.1 = (f32[8,128,256]{2,1,0:T(8,128)S(1)}, f32[8,128,256]{2,1,0:T(8,128)S(1)}) custom-call(s32[1]{0:T(128)} %bitcast.2.me_ref, s32[1,160]{1,0:T(1,128)S(1)} %copy-done.8, s32[1,160]{1,0:T(1,128)S(1)} %copy-done.9, s32[1,1]{1,0:T(1,128)S(6)} %copy.16.count_ref, f32[1,4,128,128]{3,2,1,0:T(8,128)S(1)} %copy-done.3, ...), custom_call_target="tpu_custom_call" | custom-call | flops 1610612736 | bytes 10485760 | tf_op jit(solution)/shard_map/leaf_to_parents/pallas_call | solution.py:155
  13.6 0.6 collective-permute-start
  14.2 0.1 slice_bitcast_fusion.6
  14.2 2.2 %collective-permute-done = f32[8,128,256]{2,1,0:T(8,128)S(1)} collective-permute-done((f32[8,128,256]{2,1,0:T(8,128)S(1)}, f32[8,128,256]{2,1,0:T(8,128)S(1)}, u32[]{:S(2)}, u32[]{:S(2)}) %collective-permute-start) | collective-permute-done | bytes 1048608 | tf_op jit(solution)/shard_map/ppermute | solution.py:297
  16.5 0.1 slice_bitcast_fusion.2
  16.5 0.0 copy-start.5
  16.5 0.0 copy-start.6
  16.6 0.1 slice_add_fusion.7
  16.6 5.3 %collective-permute-start.1 = (f32[1,2,128,256]{3,2,1,0:T(8,128)S(1)}, f32[1,2,128,256]{3,2,1,0:T(8,128)S(1)}, u32[]{:S(2)}, u32[]{:S(2)}) collective-permute-start(f32[1,2,128,256]{3,2,1,0:T(8,128)S(1)} %get-tuple-element.37), channel_id=1, source_target_pairs={{0,2},{1,3},{2,0},{3,1},{4,6},{5,7},{6,4},{7,5},{8,10},{9,11},{10,... | collective-permute-start | bytes 786440 | tf_op jit(solution)/shard_map/ppermute | solution.py:297
  22.0 0.1 slice_add_fusion.5
  22.0 1.5 %collective-permute-start.3 = (f32[1,2,128,256]{3,2,1,0:T(8,128)S(1)}, f32[1,2,128,256]{3,2,1,0:T(8,128)S(1)}, u32[]{:S(2)}, u32[]{:S(2)}) collective-permute-start(f32[1,2,128,256]{3,2,1,0:T(8,128)S(1)} %get-tuple-element.31), channel_id=1, source_target_pairs={{0,4},{1,5},{2,6},{3,7},{4,0},{5,1},{6,2},{7,3},{8,12},{9,13},{10,... | collective-permute-start | bytes 786440 | tf_op jit(solution)/shard_map/ppermute | solution.py:297
  24.2 1.9 %parent_sums.1 = (bf16[16,128,256]{2,1,0:T(8,128)(2,1)S(1)}, bf16[16,128,256]{2,1,0:T(8,128)(2,1)S(1)}, f32[2,64,128]{2,1,0:T(8,128)S(1)}) custom-call(s32[1]{0:T(128)} %bitcast.2.me_ref, s32[1,80]{1,0:T(1,128)S(1)} %copy-done.10, s32[1,80]{1,0:T(1,128)S(1)} %copy-done.11, s32[1,1]{1,0:T(1,128)S(6)} %copy.17.count_ref, f32[1,80,128,128]{3,2,1,0:T(8,128)S(1)} %copy-done.1, ...), custom_call_target="tpu_custom_call" | custom-call | flops 1310720 | bytes 5242880 | tf_op jit(solution)/shard_map/parent_sums/pallas_call | solution.py:204
  26.1 2.7 %collective-permute-done.1 = f32[1,2,128,256]{3,2,1,0:T(8,128)S(1)} collective-permute-done((f32[1,2,128,256]{3,2,1,0:T(8,128)S(1)}, f32[1,2,128,256]{3,2,1,0:T(8,128)S(1)}, u32[]{:S(2)}, u32[]{:S(2)}) %collective-permute-start.1) | collective-permute-done | bytes 262176 | tf_op jit(solution)/shard_map/ppermute | solution.py:297
  28.9 1.5 %collective-permute-start.2 = (f32[1,1,128,256]{3,2,1,0:T(8,128)S(1)}, f32[1,1,128,256]{3,2,1,0:T(8,128)S(1)}, u32[]{:S(2)}, u32[]{:S(2)}) collective-permute-start(f32[1,1,128,256]{3,2,1,0:T(8,128)S(1)} %get-tuple-element.44), channel_id=1, source_target_pairs={{0,4},{1,5},{2,6},{3,7},{4,0},{5,1},{6,2},{7,3},{8,12},{9,13},{10,... | collective-permute-start | bytes 393224 | tf_op jit(solution)/shard_map/ppermute | solution.py:297
  30.3 0.1 collective-permute-done.3
  30.5 1.7 %collective-permute-start.4 = (f32[1,1,128,256]{3,2,1,0:T(8,128)S(1)}, f32[1,1,128,256]{3,2,1,0:T(8,128)S(1)}, u32[]{:S(2)}, u32[]{:S(2)}) collective-permute-start(f32[1,1,128,256]{3,2,1,0:T(8,128)S(1)} %get-tuple-element.42), channel_id=1, source_target_pairs={{0,2},{1,3},{2,0},{3,1},{4,6},{5,7},{6,4},{7,5},{8,10},{9,11},{10,... | collective-permute-start | bytes 393224 | tf_op jit(solution)/shard_map/ppermute | solution.py:297
  32.2 4.9 %leaf_to_tops.1 = (f32[8,128,256]{2,1,0:T(8,128)S(1)}, f32[8,128,256]{2,1,0:T(8,128)S(1)}) custom-call(s32[1]{0:T(128)} %bitcast.2.me_ref, s32[1,160]{1,0:T(1,128)S(1)} %copy-done.8, s32[1,160]{1,0:T(1,128)S(1)} %copy-done.9, s32[1,1]{1,0:T(1,128)S(6)} %copy.16.count_ref, f32[1,4,128,128]{3,2,1,0:T(8,128)S(1)} %copy-done.3, ...), custom_call_target="tpu_custom_call" | custom-call | flops 1610612736 | bytes 10485760 | tf_op jit(solution)/shard_map/leaf_to_tops/pallas_call | solution.py:155
  37.1 0.0 collective-permute-done.2
  37.1 0.0 collective-permute-done.4
  37.2 2.1 %parent_products.1 = (f32[2,128,256]{2,1,0:T(8,128)}, f32[8,128,256]{2,1,0:T(8,128)S(1)}, f32[8,128,256]{2,1,0:T(8,128)S(1)}) custom-call(f32[2,128,256]{2,1,0:T(8,128)S(1)} %bitcast.54, f32[2,128,128]{2,1,0:T(8,128)S(1)} %bitcast.55, bf16[16,128,256]{2,1,0:T(8,128)(2,1)S(1)} %get-tuple-element.12.high_ref, ...), custom_call_target="tpu_custom_call" | custom-call | flops 805306368 | bytes 2097152 | tf_op jit(solution)/shard_map/parent_products/pallas_call | solution.py:253
  39.3 0.0 collective-permute-start.5
  39.3 0.1 slice_bitcast_fusion.4
  39.4 2.6 %collective-permute-done.5 = f32[8,128,256]{2,1,0:T(8,128)S(1)} collective-permute-done((f32[8,128,256]{2,1,0:T(8,128)S(1)}, f32[8,128,256]{2,1,0:T(8,128)S(1)}, u32[]{:S(2)}, u32[]{:S(2)}) %collective-permute-start.5) | collective-permute-done | bytes 1048608 | tf_op jit(solution)/shard_map/ppermute | solution.py:297
  42.0 0.1 slice_bitcast_fusion
  42.0 0.1 slice_add_fusion.3
  42.1 2.1 %collective-permute-start.6 = (f32[1,2,128,256]{3,2,1,0:T(8,128)S(1)}, f32[1,2,128,256]{3,2,1,0:T(8,128)S(1)}, u32[]{:S(2)}, u32[]{:S(2)}) collective-permute-start(f32[1,2,128,256]{3,2,1,0:T(8,128)S(1)} %get-tuple-element.29), channel_id=1, source_target_pairs={{0,2},{1,3},{2,0},{3,1},{4,6},{5,7},{6,4},{7,5},{8,10},{9,11},{10,... | collective-permute-start | bytes 786440 | tf_op jit(solution)/shard_map/ppermute | solution.py:297
  44.2 0.1 slice_add_fusion.1
  44.3 1.4 %collective-permute-start.8 = (f32[1,2,128,256]{3,2,1,0:T(8,128)S(1)}, f32[1,2,128,256]{3,2,1,0:T(8,128)S(1)}, u32[]{:S(2)}, u32[]{:S(2)}) collective-permute-start(f32[1,2,128,256]{3,2,1,0:T(8,128)S(1)} %get-tuple-element.23), channel_id=1, source_target_pairs={{0,4},{1,5},{2,6},{3,7},{4,0},{5,1},{6,2},{7,3},{8,12},{9,13},{10,... | collective-permute-start | bytes 786440 | tf_op jit(solution)/shard_map/ppermute | solution.py:297
  45.6 5.4 %collective-permute-done.6 = f32[1,2,128,256]{3,2,1,0:T(8,128)S(1)} collective-permute-done((f32[1,2,128,256]{3,2,1,0:T(8,128)S(1)}, f32[1,2,128,256]{3,2,1,0:T(8,128)S(1)}, u32[]{:S(2)}, u32[]{:S(2)}) %collective-permute-start.6) | collective-permute-done | bytes 262176 | tf_op jit(solution)/shard_map/ppermute | solution.py:297
  51.1 1.4 %collective-permute-start.7 = (f32[1,1,128,256]{3,2,1,0:T(8,128)S(1)}, f32[1,1,128,256]{3,2,1,0:T(8,128)S(1)}, u32[]{:S(2)}, u32[]{:S(2)}) collective-permute-start(f32[1,1,128,256]{3,2,1,0:T(8,128)S(1)} %get-tuple-element.40), channel_id=1, source_target_pairs={{0,4},{1,5},{2,6},{3,7},{4,0},{5,1},{6,2},{7,3},{8,12},{9,13},{10,... | collective-permute-start | bytes 393224 | tf_op jit(solution)/shard_map/ppermute | solution.py:297
  52.5 0.2 collective-permute-done.8
  52.7 1.6 %collective-permute-start.9 = (f32[1,1,128,256]{3,2,1,0:T(8,128)S(1)}, f32[1,1,128,256]{3,2,1,0:T(8,128)S(1)}, u32[]{:S(2)}, u32[]{:S(2)}) collective-permute-start(f32[1,1,128,256]{3,2,1,0:T(8,128)S(1)} %get-tuple-element.38), channel_id=1, source_target_pairs={{0,2},{1,3},{2,0},{3,1},{4,6},{5,7},{6,4},{7,5},{8,10},{9,11},{10,... | collective-permute-start | bytes 393224 | tf_op jit(solution)/shard_map/ppermute | solution.py:297
  54.3 2.0 %collective-permute-done.7 = f32[1,1,128,256]{3,2,1,0:T(8,128)S(1)} collective-permute-done((f32[1,1,128,256]{3,2,1,0:T(8,128)S(1)}, f32[1,1,128,256]{3,2,1,0:T(8,128)S(1)}, u32[]{:S(2)}, u32[]{:S(2)}) %collective-permute-start.7) | collective-permute-done | bytes 131104 | tf_op jit(solution)/shard_map/ppermute | solution.py:297
  56.3 1.4 %collective-permute-done.9 = f32[1,1,128,256]{3,2,1,0:T(8,128)S(1)} collective-permute-done((f32[1,1,128,256]{3,2,1,0:T(8,128)S(1)}, f32[1,1,128,256]{3,2,1,0:T(8,128)S(1)}, u32[]{:S(2)}, u32[]{:S(2)}) %collective-permute-start.9) | collective-permute-done | bytes 131104 | tf_op jit(solution)/shard_map/ppermute | solution.py:297
  57.7 0.4 top_products.1
  58.1 3.2 %collective-permute-start.10 = (f32[2,64,128]{2,1,0:T(8,128)S(1)}, f32[2,64,128]{2,1,0:T(8,128)S(1)}, u32[]{:S(2)}, u32[]{:S(2)}) collective-permute-start(f32[2,64,128]{2,1,0:T(8,128)S(1)} %get-tuple-element.46), channel_id=1, source_target_pairs={{0,8},{8,0},{16,24},{24,16},{1,9},{9,1},{17,25},{25,17},{2,10},{10... | collective-permute-start | bytes 196616 | tf_op jit(solution)/shard_map/ppermute | solution.py:297
  61.3 0.8 %collective-permute-start.12 = (f32[2,64,128]{2,1,0:T(8,128)S(1)}, f32[2,64,128]{2,1,0:T(8,128)S(1)}, u32[]{:S(2)}, u32[]{:S(2)}) collective-permute-start(f32[2,64,128]{2,1,0:T(8,128)S(1)} %get-tuple-element.47), channel_id=1, source_target_pairs={{0,24},{8,16},{16,8},{24,0},{1,25},{9,17},{17,9},{25,1},{2,26},{10... | collective-permute-start | bytes 196616 | tf_op jit(solution)/shard_map/ppermute | solution.py:297
  62.1 0.8 %collective-permute-start.11 = (f32[2,64,128]{2,1,0:T(8,128)S(1)}, f32[2,64,128]{2,1,0:T(8,128)S(1)}, u32[]{:S(2)}, u32[]{:S(2)}) collective-permute-start(f32[2,64,128]{2,1,0:T(8,128)S(1)} %get-tuple-element.48), channel_id=1, source_target_pairs={{0,16},{8,24},{16,0},{24,8},{1,17},{9,25},{17,1},{25,9},{2,18},{10... | collective-permute-start | bytes 196616 | tf_op jit(solution)/shard_map/ppermute | solution.py:297
  62.8 1.9 %collective-permute-done.10 = f32[2,64,128]{2,1,0:T(8,128)S(1)} collective-permute-done((f32[2,64,128]{2,1,0:T(8,128)S(1)}, f32[2,64,128]{2,1,0:T(8,128)S(1)}, u32[]{:S(2)}, u32[]{:S(2)}) %collective-permute-start.10) | collective-permute-done | bytes 65568 | tf_op jit(solution)/shard_map/ppermute | solution.py:297
  64.7 2.8 %collective-permute-done.12 = f32[2,64,128]{2,1,0:T(8,128)S(1)} collective-permute-done((f32[2,64,128]{2,1,0:T(8,128)S(1)}, f32[2,64,128]{2,1,0:T(8,128)S(1)}, u32[]{:S(2)}, u32[]{:S(2)}) %collective-permute-start.12) | collective-permute-done | bytes 65568 | tf_op jit(solution)/shard_map/ppermute | solution.py:297
  67.5 1.2 %collective-permute-done.11 = f32[2,64,128]{2,1,0:T(8,128)S(1)} collective-permute-done((f32[2,64,128]{2,1,0:T(8,128)S(1)}, f32[2,64,128]{2,1,0:T(8,128)S(1)}, u32[]{:S(2)}, u32[]{:S(2)}) %collective-permute-start.11) | collective-permute-done | bytes 65568 | tf_op jit(solution)/shard_map/ppermute | solution.py:297
  68.6 0.7 fusion.8
  (21 shorter events, 0.2 us)
Async XLA Ops:
  0.6 23.5 %copy-start.10 = (s32[1,80]{1,0:T(1,128)S(1)}, s32[1,80]{1,0:T(1,128)}, u32[]{:S(2)}) copy-start(s32[1,80]{1,0:T(1,128)} %rows_ref.3) | copy-start | bytes 964
  0.6 23.5 %copy-start.11 = (s32[1,80]{1,0:T(1,128)S(1)}, s32[1,80]{1,0:T(1,128)}, u32[]{:S(2)}) copy-start(s32[1,80]{1,0:T(1,128)} %cols_ref.3) | copy-start | bytes 964
  1.3 4.0 %copy-start = (f32[1,160,128,128]{3,2,1,0:T(8,128)S(1)}, f32[1,160,128,128]{3,2,1,0:T(8,128)}, u32[]{:S(2)}) copy-start(f32[1,160,128,128]{3,2,1,0:T(8,128)} %tiles_hbm.5) | copy-start | bytes 31457284
  5.3 1.0 %copy-start.2 = (f32[1,4,128,256]{3,2,1,0:T(8,128)S(1)}, f32[1,4,128,256]{3,2,1,0:T(8,128)}, u32[]{:S(2)}) copy-start(f32[1,4,128,256]{3,2,1,0:T(8,128)} %rhs_hbm.3) | copy-start | bytes 1572868
  6.3 0.9 %copy-start.3 = (f32[1,4,128,128]{3,2,1,0:T(8,128)S(1)}, f32[1,4,128,128]{3,2,1,0:T(8,128)}, u32[]{:S(2)}) copy-start(f32[1,4,128,128]{3,2,1,0:T(8,128)} %inv_hbm.3) | copy-start | bytes 786436
  7.3 0.7 copy-start.8
  8.0 0.7 copy-start.9
  8.7 15.5 %copy-start.1 = (f32[1,80,128,128]{3,2,1,0:T(8,128)S(1)}, f32[1,80,128,128]{3,2,1,0:T(8,128)}, u32[]{:S(2)}) copy-start(f32[1,80,128,128]{3,2,1,0:T(8,128)} %tiles_hbm.3) | copy-start | bytes 15728644
  8.7 15.6 %copy-start.4 = (f32[2,128,128]{2,1,0:T(8,128)S(1)}, f32[2,128,128]{2,1,0:T(8,128)}, u32[]{:S(2)}) copy-start(f32[2,128,128]{2,1,0:T(8,128)} %inv_ref.1) | copy-start | bytes 393220
  8.7 15.6 %copy-start.7 = (f32[2,128,64]{1,2,0:T(8,128)S(1)}, f32[2,128,64]{1,2,0:T(8,128)}, u32[]{:S(2)}) copy-start(f32[2,128,64]{1,2,0:T(8,128)} %param.18) | copy-start | bytes 196612
  13.6 2.9 %collective-permute-start = (f32[8,128,256]{2,1,0:T(8,128)S(1)}, f32[8,128,256]{2,1,0:T(8,128)S(1)}, u32[]{:S(2)}, u32[]{:S(2)}) collective-permute-start(f32[8,128,256]{2,1,0:T(8,128)S(1)} %get-tuple-element.17), channel_id=1, source_target_pairs={{0,1},{1,0},{2,3},{3,2},{4,5},{5,4},{6,7},{7,6},{8,9},{9,8},{10,11... | collective-permute-start | bytes 3145736 | tf_op jit(solution)/shard_map/ppermute | solution.py:297
  16.5 20.6 %copy-start.5 = (f32[1,2,128,256]{3,2,1,0:T(8,128)S(1)}, f32[1,2,128,256]{3,2,1,0:T(8,128)}, u32[]{:S(2)}) copy-start(f32[1,2,128,256]{3,2,1,0:T(8,128)} %param.16) | copy-start | bytes 786436
  16.5 20.6 %copy-start.6 = (f32[1,2,128,128]{3,2,1,0:T(8,128)S(1)}, f32[1,2,128,128]{3,2,1,0:T(8,128)}, u32[]{:S(2)}) copy-start(f32[1,2,128,128]{3,2,1,0:T(8,128)} %param.17) | copy-start | bytes 393220
  16.6 12.2 %collective-permute-start.1 = (f32[1,2,128,256]{3,2,1,0:T(8,128)S(1)}, f32[1,2,128,256]{3,2,1,0:T(8,128)S(1)}, u32[]{:S(2)}, u32[]{:S(2)}) collective-permute-start(f32[1,2,128,256]{3,2,1,0:T(8,128)S(1)} %get-tuple-element.37), channel_id=1, source_target_pairs={{0,2},{1,3},{2,0},{3,1},{4,6},{5,7},{6,4},{7,5},{8,10},{9,11},{10,... | collective-permute-start | bytes 786440 | tf_op jit(solution)/shard_map/ppermute | solution.py:297
  22.0 8.4 %collective-permute-start.3 = (f32[1,2,128,256]{3,2,1,0:T(8,128)S(1)}, f32[1,2,128,256]{3,2,1,0:T(8,128)S(1)}, u32[]{:S(2)}, u32[]{:S(2)}) collective-permute-start(f32[1,2,128,256]{3,2,1,0:T(8,128)S(1)} %get-tuple-element.31), channel_id=1, source_target_pairs={{0,4},{1,5},{2,6},{3,7},{4,0},{5,1},{6,2},{7,3},{8,12},{9,13},{10,... | collective-permute-start | bytes 786440 | tf_op jit(solution)/shard_map/ppermute | solution.py:297
  28.9 8.3 %collective-permute-start.2 = (f32[1,1,128,256]{3,2,1,0:T(8,128)S(1)}, f32[1,1,128,256]{3,2,1,0:T(8,128)S(1)}, u32[]{:S(2)}, u32[]{:S(2)}) collective-permute-start(f32[1,1,128,256]{3,2,1,0:T(8,128)S(1)} %get-tuple-element.44), channel_id=1, source_target_pairs={{0,4},{1,5},{2,6},{3,7},{4,0},{5,1},{6,2},{7,3},{8,12},{9,13},{10,... | collective-permute-start | bytes 393224 | tf_op jit(solution)/shard_map/ppermute | solution.py:297
  30.5 6.7 %collective-permute-start.4 = (f32[1,1,128,256]{3,2,1,0:T(8,128)S(1)}, f32[1,1,128,256]{3,2,1,0:T(8,128)S(1)}, u32[]{:S(2)}, u32[]{:S(2)}) collective-permute-start(f32[1,1,128,256]{3,2,1,0:T(8,128)S(1)} %get-tuple-element.42), channel_id=1, source_target_pairs={{0,2},{1,3},{2,0},{3,1},{4,6},{5,7},{6,4},{7,5},{8,10},{9,11},{10,... | collective-permute-start | bytes 393224 | tf_op jit(solution)/shard_map/ppermute | solution.py:297
  39.3 2.7 %collective-permute-start.5 = (f32[8,128,256]{2,1,0:T(8,128)S(1)}, f32[8,128,256]{2,1,0:T(8,128)S(1)}, u32[]{:S(2)}, u32[]{:S(2)}) collective-permute-start(f32[8,128,256]{2,1,0:T(8,128)S(1)} %get-tuple-element.21), channel_id=1, source_target_pairs={{0,1},{1,0},{2,3},{3,2},{4,5},{5,4},{6,7},{7,6},{8,9},{9,8},{10,11... | collective-permute-start | bytes 3145736 | tf_op jit(solution)/shard_map/ppermute | solution.py:297
  42.1 8.9 %collective-permute-start.6 = (f32[1,2,128,256]{3,2,1,0:T(8,128)S(1)}, f32[1,2,128,256]{3,2,1,0:T(8,128)S(1)}, u32[]{:S(2)}, u32[]{:S(2)}) collective-permute-start(f32[1,2,128,256]{3,2,1,0:T(8,128)S(1)} %get-tuple-element.29), channel_id=1, source_target_pairs={{0,2},{1,3},{2,0},{3,1},{4,6},{5,7},{6,4},{7,5},{8,10},{9,11},{10,... | collective-permute-start | bytes 786440 | tf_op jit(solution)/shard_map/ppermute | solution.py:297
  44.3 8.4 %collective-permute-start.8 = (f32[1,2,128,256]{3,2,1,0:T(8,128)S(1)}, f32[1,2,128,256]{3,2,1,0:T(8,128)S(1)}, u32[]{:S(2)}, u32[]{:S(2)}) collective-permute-start(f32[1,2,128,256]{3,2,1,0:T(8,128)S(1)} %get-tuple-element.23), channel_id=1, source_target_pairs={{0,4},{1,5},{2,6},{3,7},{4,0},{5,1},{6,2},{7,3},{8,12},{9,13},{10,... | collective-permute-start | bytes 786440 | tf_op jit(solution)/shard_map/ppermute | solution.py:297
  51.1 5.3 %collective-permute-start.7 = (f32[1,1,128,256]{3,2,1,0:T(8,128)S(1)}, f32[1,1,128,256]{3,2,1,0:T(8,128)S(1)}, u32[]{:S(2)}, u32[]{:S(2)}) collective-permute-start(f32[1,1,128,256]{3,2,1,0:T(8,128)S(1)} %get-tuple-element.40), channel_id=1, source_target_pairs={{0,4},{1,5},{2,6},{3,7},{4,0},{5,1},{6,2},{7,3},{8,12},{9,13},{10,... | collective-permute-start | bytes 393224 | tf_op jit(solution)/shard_map/ppermute | solution.py:297
  52.7 5.0 %collective-permute-start.9 = (f32[1,1,128,256]{3,2,1,0:T(8,128)S(1)}, f32[1,1,128,256]{3,2,1,0:T(8,128)S(1)}, u32[]{:S(2)}, u32[]{:S(2)}) collective-permute-start(f32[1,1,128,256]{3,2,1,0:T(8,128)S(1)} %get-tuple-element.38), channel_id=1, source_target_pairs={{0,2},{1,3},{2,0},{3,1},{4,6},{5,7},{6,4},{7,5},{8,10},{9,11},{10,... | collective-permute-start | bytes 393224 | tf_op jit(solution)/shard_map/ppermute | solution.py:297
  58.1 6.6 %collective-permute-start.10 = (f32[2,64,128]{2,1,0:T(8,128)S(1)}, f32[2,64,128]{2,1,0:T(8,128)S(1)}, u32[]{:S(2)}, u32[]{:S(2)}) collective-permute-start(f32[2,64,128]{2,1,0:T(8,128)S(1)} %get-tuple-element.46), channel_id=1, source_target_pairs={{0,8},{8,0},{16,24},{24,16},{1,9},{9,1},{17,25},{25,17},{2,10},{10... | collective-permute-start | bytes 196616 | tf_op jit(solution)/shard_map/ppermute | solution.py:297
  61.3 6.2 %collective-permute-start.12 = (f32[2,64,128]{2,1,0:T(8,128)S(1)}, f32[2,64,128]{2,1,0:T(8,128)S(1)}, u32[]{:S(2)}, u32[]{:S(2)}) collective-permute-start(f32[2,64,128]{2,1,0:T(8,128)S(1)} %get-tuple-element.47), channel_id=1, source_target_pairs={{0,24},{8,16},{16,8},{24,0},{1,25},{9,17},{17,9},{25,1},{2,26},{10... | collective-permute-start | bytes 196616 | tf_op jit(solution)/shard_map/ppermute | solution.py:297
  62.1 6.6 %collective-permute-start.11 = (f32[2,64,128]{2,1,0:T(8,128)S(1)}, f32[2,64,128]{2,1,0:T(8,128)S(1)}, u32[]{:S(2)}, u32[]{:S(2)}) collective-permute-start(f32[2,64,128]{2,1,0:T(8,128)S(1)} %get-tuple-element.48), channel_id=1, source_target_pairs={{0,16},{8,24},{16,0},{24,8},{1,17},{9,25},{17,1},{25,9},{2,18},{10... | collective-permute-start | bytes 196616 | tf_op jit(solution)/shard_map/ppermute | solution.py:297
